TPU v7x, 32 devices: a whole 2x2x4 slice. The times are simulated.
32 devices in a mesh: shard: 2 (over x), ctx: 4 (over y, core), tp: 4 (over z).
Axes of the slice: x: 2, y: 2, z: 4, core: 2. Of those that a mesh axis runs over, the one named last changes fastest.
Arguments:
- hidden_in: bfloat16 [4, 1024, 1024], P('shard', 'ctx'), may hold values from -6 to 6
- lengths: int32 [4], P('shard'), may hold values from 1 to 1024, as said below
- cotangent: bfloat16 [4, 1024, 1024], P('shard', 'ctx'), may hold values from -6 to 6
- ln1_gain: bfloat16 [1024], P(('shard', 'ctx')), may hold values from 0.5 to 1.5
- ln1_bias: bfloat16 [1024], P(('shard', 'ctx')), may hold values from -3 to 3
- w_qkv: bfloat16 [3, 1024, 1024], P(None, ('shard', 'ctx'), 'tp'), may hold values from -0.1875 to 0.1875
- b_qv: bfloat16 [2, 1024], P(None, 'tp'), may hold values from -3 to 3
- w_out: bfloat16 [1024, 1024], P(('shard', 'ctx'), 'tp'), may hold values from -1.5 to 1.5
- b_out: bfloat16 [1024], P(('shard', 'ctx')), may hold values from -3 to 3
- ln2_gain: bfloat16 [1024], P(('shard', 'ctx')), may hold values from 0.5 to 1.5
- ln2_bias: bfloat16 [1024], P(('shard', 'ctx')), may hold values from -3 to 3
- w_up: bfloat16 [1024, 4096], P(('shard', 'ctx'), 'tp'), may hold values from -0.1875 to 0.1875
- b_up: bfloat16 [4096], P('tp'), may hold values from -3 to 3
- w_down: bfloat16 [1024, 4096], P(('shard', 'ctx'), 'tp'), may hold values from -0.375 to 0.375
- b_down: bfloat16 [1024], P(('shard', 'ctx')), may hold values from -3 to 3
Outputs:
- hidden_out: float32 [4, 1024, 1024], P('shard', 'ctx')
- grad_in: float32 [4, 1024, 1024], P('shard', 'ctx')
- grad_ln1_gain: float32 [1024], P(('shard', 'ctx'))
- grad_ln1_bias: float32 [1024], P(('shard', 'ctx'))
- grad_w_qkv: float32 [3, 1024, 1024], P(None, ('shard', 'ctx'), 'tp')
- grad_b_qv: float32 [2, 1024], P(None, 'tp')
- grad_w_out: float32 [1024, 1024], P(('shard', 'ctx'), 'tp')
- grad_b_out: float32 [1024], P(('shard', 'ctx'))
- grad_ln2_gain: float32 [1024], P(('shard', 'ctx'))
- grad_ln2_bias: float32 [1024], P(('shard', 'ctx'))
- grad_w_up: float32 [1024, 4096], P(('shard', 'ctx'), 'tp')
- grad_b_up: float32 [4096], P('tp')
- grad_w_down: float32 [1024, 4096], P(('shard', 'ctx'), 'tp')
- grad_b_down: float32 [1024], P(('shard', 'ctx'))
Inputs may be any that keep to these rules, and one draw needn't show every extreme that they name: Sequence i belongs to shard group i // 2; its positions from lengths[i] on are padding. Some sequence has all 1024 positions live.
All inputs are finite; a program needn't handle non-finite values.
Results may differ from a plain program's by a relative error of at most 0.012.
The roundings to bfloat16 on the way count: a program that leaves them out, or rounds other values in their place, can miss the bound.
Values may be sent and summed in bfloat16 or wider, within the bound.
A program may use at most 128 MiB of HBM per device.

v0:
```python
import math
import jax
import jax.numpy as jnp
from jax import lax
from jax.sharding import PartitionSpec as P

HD = 64
EPS = 1e-05
KAPPA = math.sqrt(2.0 / math.pi)


def normalize(row, gain, shift):
    center = jnp.mean(row, axis=-1, keepdims=True)
    centred = row - center
    inv_std = lax.rsqrt(jnp.mean(centred * centred, axis=-1, keepdims=True) + EPS)
    unit_rows = centred * inv_std
    return (unit_rows * gain + shift, unit_rows, inv_std)


def normalize_back(grad_out, unit_rows, inv_std, gain):
    scaled = grad_out * gain
    return inv_std * (
        scaled
        - jnp.mean(scaled, axis=-1, keepdims=True)
        - unit_rows * jnp.mean(scaled * unit_rows, axis=-1, keepdims=True)
    )


def gelu_pair(pre_act):
    inner = KAPPA * (pre_act + 0.044715 * pre_act * pre_act * pre_act)
    tanh_val = jnp.tanh(inner)
    value_out = 0.5 * pre_act * (1.0 + tanh_val)
    slope = 0.5 * (1.0 + tanh_val) + 0.5 * pre_act * (1.0 - tanh_val * tanh_val) * KAPPA * (
        1.0 + 3.0 * 0.044715 * pre_act * pre_act
    )
    return (value_out, slope)


def contract_last(left, right):
    return lax.dot_general(
        left, right, (((1,), (1,)), ((), ())), preferred_element_type=jnp.float32
    )


def contract_first(left, right):
    return lax.dot_general(
        left, right, (((0,), (0,)), ((), ())), preferred_element_type=jnp.float32
    )


def on_device(
    hidden_in,
    lengths,
    cotangent,
    ln1_gain,
    ln1_bias,
    w_qkv,
    b_qv,
    w_out,
    b_out,
    ln2_gain,
    ln2_bias,
    w_up,
    b_up,
    w_down,
    b_down,
):
    groups, block_len, width = hidden_in.shape
    head_width = w_qkv.shape[2]
    heads_here = head_width // HD
    row_count = groups * block_len
    scale = 1.0 / math.sqrt(HD)
    vectors = jnp.stack([ln1_gain, ln1_bias, b_out, ln2_gain, ln2_bias, b_down], 0)
    fetched = (
        lax.all_gather(w_qkv, ("shard", "ctx"), axis=1, tiled=True),
        lax.all_gather(w_out, ("shard", "ctx"), axis=0, tiled=True),
        lax.all_gather(w_up, ("shard", "ctx"), axis=0, tiled=True),
        lax.all_gather(w_down, ("shard", "ctx"), axis=0, tiled=True),
        lax.all_gather(vectors, ("shard", "ctx"), axis=1, tiled=True),
    )
    qkv_full, out_full, up_full, down_full, vec_full = fetched
    vec_wide = vec_full.astype(jnp.float32)
    gain_one = vec_wide[0]
    shift_one = vec_wide[1]
    bias_out = vec_wide[2]
    gain_two = vec_wide[3]
    shift_two = vec_wide[4]
    bias_down = vec_wide[5]
    ctx_index = lax.axis_index("ctx")
    positions = jnp.arange(block_len, dtype=jnp.int32) + ctx_index * block_len
    live_rows = (positions[None, :] < lengths[:, None]).reshape(row_count, 1)

    def allowed_mask(start, count):
        key_pos = start + jnp.arange(count, dtype=jnp.int32)
        causal = key_pos[None, None, None, :] <= positions[None, None, :, None]
        inside = key_pos[None, None, None, :] < lengths[:, None, None, None]
        return causal & inside

    inputs = hidden_in.reshape(row_count, width).astype(jnp.float32)
    normed_one, unit_one, inv_one = normalize(inputs, gain_one, shift_one)
    normed_bf = normed_one.astype(jnp.bfloat16)
    projected = jnp.einsum("rd,jde->jre", normed_bf, qkv_full, preferred_element_type=jnp.float32)
    query = (projected[0] + b_qv[0].astype(jnp.float32)).astype(jnp.bfloat16)
    keys_here = projected[1].astype(jnp.bfloat16).reshape(groups, block_len, head_width)
    values_here = (
        (projected[2] + b_qv[1].astype(jnp.float32))
        .astype(jnp.bfloat16)
        .reshape(groups, block_len, head_width)
    )
    query_heads = query.reshape(groups, block_len, heads_here, HD)

    def fold_keys(step_fn, init):
        return step_fn(
            init,
            (
                lax.all_gather(keys_here, "ctx", axis=1, tiled=True),
                lax.all_gather(values_here, "ctx", axis=1, tiled=True),
            ),
            jnp.int32(0),
        )

    def piece_scores(piece, start):
        key_piece, value_piece = piece
        count = key_piece.shape[1]
        key_heads = key_piece.reshape(groups, count, heads_here, HD)
        value_heads = value_piece.reshape(groups, count, heads_here, HD)
        scores = (
            jnp.einsum(
                "sqhd,skhd->shqk", query_heads, key_heads, preferred_element_type=jnp.float32
            )
            * scale
        )
        allowed = allowed_mask(start, count)
        return (jnp.where(allowed, scores, -1e30), allowed, value_heads)

    def totals_step(carry, piece, start):
        top, total = carry
        scores, allowed, unused = piece_scores(piece, start)
        new_top = jnp.maximum(top, jnp.max(scores, axis=-1))
        weights = jnp.where(allowed, jnp.exp(scores - new_top[..., None]), 0.0)
        total = jnp.sum(weights, axis=-1)
        return (new_top, total)

    start_totals = (
        jnp.full((groups, heads_here, block_len), -1e30, jnp.float32),
        jnp.zeros((groups, heads_here, block_len), jnp.float32),
    )
    top, total = fold_keys(totals_step, start_totals)
    log_total = top + jnp.log(total)

    def values_step(accum, piece, start):
        scores, allowed, value_heads = piece_scores(piece, start)
        probs_piece = jnp.where(allowed, jnp.exp(scores - log_total[..., None]), 0.0).astype(
            jnp.bfloat16
        )
        return jnp.einsum(
            "shqk,skhd->sqhd", probs_piece, value_heads, preferred_element_type=jnp.float32
        )

    accum = fold_keys(values_step, jnp.zeros((groups, block_len, heads_here, HD), jnp.float32))
    attended_heads = accum.astype(jnp.bfloat16)
    attended = attended_heads.reshape(row_count, head_width)
    proj_sum = lax.psum(contract_last(attended, out_full), "tp")
    resid = inputs + proj_sum + bias_out
    normed_two, unit_two, inv_two = normalize(resid, gain_two, shift_two)
    second_bf = normed_two.astype(jnp.bfloat16)
    pre_act = jnp.dot(second_bf, up_full, preferred_element_type=jnp.float32) + b_up.astype(
        jnp.float32
    )
    activ, slope = gelu_pair(pre_act)
    hidden = activ.astype(jnp.bfloat16)
    mlp_sum = lax.psum(contract_last(hidden, down_full), "tp")
    result = jnp.where(live_rows, resid + mlp_sum + bias_down, 0.0)
    again = (
        lax.all_gather(w_qkv, ("shard", "ctx"), axis=1, tiled=True),
        lax.all_gather(w_out, ("shard", "ctx"), axis=0, tiled=True),
        lax.all_gather(w_up, ("shard", "ctx"), axis=0, tiled=True),
        lax.all_gather(w_down, ("shard", "ctx"), axis=0, tiled=True),
    )
    qkv_back, out_back, up_back, down_back = again
    grad_rows = jnp.where(live_rows, cotangent.reshape(row_count, width).astype(jnp.float32), 0.0)
    grad_bf = grad_rows.astype(jnp.bfloat16)
    grad_bias_down = jnp.sum(grad_rows, axis=0)
    grad_down = contract_first(grad_bf, hidden)
    d_pre = jnp.dot(grad_bf, down_back, preferred_element_type=jnp.float32) * slope
    d_pre_bf = d_pre.astype(jnp.bfloat16)
    grad_bias_up = jnp.sum(d_pre, axis=0)
    grad_up = contract_first(second_bf, d_pre_bf)
    back_two = lax.psum(contract_last(d_pre_bf, up_back), "tp")
    grad_gain_two = jnp.sum(back_two * unit_two, axis=0)
    grad_shift_two = jnp.sum(back_two, axis=0)
    d_resid = grad_rows + normalize_back(back_two, unit_two, inv_two, gain_two)
    d_resid_bf = d_resid.astype(jnp.bfloat16)
    grad_bias_out = jnp.sum(d_resid, axis=0)
    grad_out = contract_first(d_resid_bf, attended)
    d_attended = jnp.dot(d_resid_bf, out_back, preferred_element_type=jnp.float32).astype(
        jnp.bfloat16
    )
    keys_whole, values_whole = (
        lax.all_gather(keys_here, "ctx", axis=1, tiled=True),
        lax.all_gather(values_here, "ctx", axis=1, tiled=True),
    )
    seq_len = keys_whole.shape[1]
    key_heads = keys_whole.reshape(groups, seq_len, heads_here, HD)
    value_heads = values_whole.reshape(groups, seq_len, heads_here, HD)
    scores = (
        jnp.einsum("sqhd,skhd->shqk", query_heads, key_heads, preferred_element_type=jnp.float32)
        * scale
    )
    allowed = allowed_mask(0, seq_len)
    exact_probs = jnp.where(allowed, jnp.exp(scores - log_total[..., None]), 0.0)
    d_att_heads = d_attended.reshape(groups, block_len, heads_here, HD)
    delta = jnp.transpose(
        jnp.sum(d_att_heads.astype(jnp.float32) * attended_heads.astype(jnp.float32), axis=-1),
        (0, 2, 1),
    )
    d_probs = jnp.einsum(
        "sqhd,skhd->shqk", d_att_heads, value_heads, preferred_element_type=jnp.float32
    )
    d_scores = (exact_probs * (d_probs - delta[..., None])).astype(jnp.bfloat16)
    d_query = (
        jnp.einsum("shqk,skhd->sqhd", d_scores, key_heads, preferred_element_type=jnp.float32)
        * scale
    )
    probs_bf = exact_probs.astype(jnp.bfloat16)
    key_terms = (
        jnp.einsum("shqk,sqhd->skhd", d_scores, query_heads, preferred_element_type=jnp.float32)
        * scale
    )
    value_terms = jnp.einsum(
        "shqk,sqhd->skhd", probs_bf, d_att_heads, preferred_element_type=jnp.float32
    )
    d_keys, d_values = (
        lax.psum_scatter(
            key_terms.reshape(groups, seq_len, head_width), "ctx", scatter_dimension=1, tiled=True
        ),
        lax.psum_scatter(
            value_terms.reshape(groups, seq_len, head_width), "ctx", scatter_dimension=1, tiled=True
        ),
    )
    d_query_rows = d_query.reshape(row_count, head_width)
    d_value_rows = d_values.reshape(row_count, head_width)
    grad_bias_qv = jnp.stack([jnp.sum(d_query_rows, axis=0), jnp.sum(d_value_rows, axis=0)], 0)
    stacked = jnp.stack(
        [d_query_rows, d_keys.reshape(row_count, head_width), d_value_rows], 0
    ).astype(jnp.bfloat16)
    grad_qkv = jnp.einsum("rd,jre->jde", normed_bf, stacked, preferred_element_type=jnp.float32)
    back_one = lax.psum(
        jnp.einsum("jre,jde->rd", stacked, qkv_back, preferred_element_type=jnp.float32), "tp"
    )
    grad_gain_one = jnp.sum(back_one * unit_one, axis=0)
    grad_shift_one = jnp.sum(back_one, axis=0)
    d_inputs = d_resid + normalize_back(back_one, unit_one, inv_one, gain_one)
    vec_grads = jnp.stack(
        [
            grad_gain_one,
            grad_shift_one,
            grad_bias_out,
            grad_gain_two,
            grad_shift_two,
            grad_bias_down,
        ],
        0,
    )
    summed = (
        lax.psum_scatter(grad_qkv, ("shard", "ctx"), scatter_dimension=1, tiled=True),
        lax.psum_scatter(grad_out, ("shard", "ctx"), scatter_dimension=0, tiled=True),
        lax.psum_scatter(grad_up, ("shard", "ctx"), scatter_dimension=0, tiled=True),
        lax.psum_scatter(grad_down, ("shard", "ctx"), scatter_dimension=0, tiled=True),
        lax.psum_scatter(vec_grads, ("shard", "ctx"), scatter_dimension=1, tiled=True),
    )
    sum_qkv, sum_out, sum_up, sum_down, sum_vec = summed
    bias_qv_sum, bias_up_sum = lax.psum((grad_bias_qv, grad_bias_up), ("shard", "ctx"))
    return (
        result.reshape(groups, block_len, width),
        d_inputs.reshape(groups, block_len, width),
        sum_vec[0],
        sum_vec[1],
        sum_qkv,
        bias_qv_sum,
        sum_out,
        sum_vec[2],
        sum_vec[3],
        sum_vec[4],
        sum_up,
        bias_up_sum,
        sum_down,
        sum_vec[5],
    )


def solution(mesh):
    return jax.shard_map(
        on_device,
        mesh=mesh,
        in_specs=(
            P("shard", "ctx", None),
            P("shard"),
            P("shard", "ctx", None),
            P(("shard", "ctx")),
            P(("shard", "ctx")),
            P(None, ("shard", "ctx"), "tp"),
            P(None, "tp"),
            P(("shard", "ctx"), "tp"),
            P(("shard", "ctx")),
            P(("shard", "ctx")),
            P(("shard", "ctx")),
            P(("shard", "ctx"), "tp"),
            P("tp"),
            P(("shard", "ctx"), "tp"),
            P(("shard", "ctx")),
        ),
        out_specs=(
            P("shard", "ctx", None),
            P("shard", "ctx", None),
            P(("shard", "ctx")),
            P(("shard", "ctx")),
            P(None, ("shard", "ctx"), "tp"),
            P(None, "tp"),
            P(("shard", "ctx"), "tp"),
            P(("shard", "ctx")),
            P(("shard", "ctx")),
            P(("shard", "ctx")),
            P(("shard", "ctx"), "tp"),
            P("tp"),
            P(("shard", "ctx"), "tp"),
            P(("shard", "ctx")),
        ),
        check_vma=False,
    )
```

profile of v0, /device:TPU:0, one launch (start us, length us, event | category | flops | bytes accessed | tf_op | source)
XLA Modules:
  0.0 817.6 jit_solution(358480449158023805)
XLA Ops:
  11.3 10.3 %all_gather.28 = bf16[6,1024]{1,0:T(8,128)(2,1)S(1)} all-gather(bf16[6,128]{1,0:T(8,128)(2,1)S(1)} %stack.61), channel_id=1, replica_groups=mesh['shard'=2,'ctx'=4,'tp'=4] {'shard','ctx'}, dimensions={1}, use_global_device_ids=true | all-gather | bytes 13824 | tf_op jit(solution)/shard_map/all_gather | solution.py:79
  23.1 15.3 %all-gather.6.cloned.1.call-done = bf16[3,1024,256]{2,1,0:T(8,128)(2,1)} async-done(((bf16[3,128,256]{2,1,0:T(8,128)(2,1)}), bf16[3,1024,256]{2,1,0:T(8,128)(2,1)}) %all-gather.6.cloned.1.call-update) | async-done | bytes 1572880 | tf_op jit(solution)/shard_map/all_gather | solution.py:75
  42.1 10.8 %all_gather.32 = bf16[1024,256]{1,0:T(8,128)(2,1)} all-gather(bf16[128,256]{1,0:T(8,128)(2,1)S(1)} %copy-done.20), channel_id=1, replica_groups=mesh['shard'=2,'ctx'=4,'tp'=4] {'shard','ctx'}, dimensions={0}, use_global_device_ids=true | all-gather | bytes 589824 | tf_op jit(solution)/shard_map/all_gather | solution.py:76
  65.4 12.3 %all-gather.8.cloned.1.call-done = bf16[2,1024,256]{2,1,0:T(8,128)(2,1)} async-done(((bf16[2,256,256]{2,1,0:T(8,128)(2,1)}), bf16[2,1024,256]{2,1,0:T(8,128)(2,1)}) %all-gather.8.cloned.1.call-update) | async-done | bytes 1048592 | tf_op jit(solution)/shard_map/all_gather | solution.py:117
  79.3 6.0 fusion.31
  90.5 83.9 %all-reduce.6.cloned.1.call-done = f32[512,1024]{1,0:T(8,128)} async-done(((f32[512,1024]{1,0:T(8,128)}), f32[512,1024]{1,0:T(8,128)}) %all-reduce.6.cloned.1.call-update) | async-done | bytes 2097168 | tf_op jit(solution)/shard_map/psum | solution.py:163
  176.8 26.5 %all-gather.12.cloned.1.call-done = bf16[1024,1024]{1,0:T(8,128)(2,1)} async-done(((bf16[128,1024]{1,0:T(8,128)(2,1)}), bf16[1024,1024]{1,0:T(8,128)(2,1)}) %all-gather.12.cloned.1.call-update) | async-done | bytes 2097168 | tf_op jit(solution)/shard_map/all_gather | solution.py:77
  207.5 25.6 %all-gather.14.cloned.1.call-done = bf16[1024,1024]{1,0:T(8,128)(2,1)} async-done(((bf16[128,1024]{1,0:T(8,128)(2,1)}), bf16[1024,1024]{1,0:T(8,128)(2,1)}) %all-gather.14.cloned.1.call-update) | async-done | bytes 2097168 | tf_op jit(solution)/shard_map/all_gather | solution.py:78
  233.1 5.0 fusion.60
  241.9 86.6 %all-reduce.8.cloned.1.call-done = f32[512,1024]{1,0:T(8,128)} async-done(((f32[512,1024]{1,0:T(8,128)}), f32[512,1024]{1,0:T(8,128)}) %all-reduce.8.cloned.1.call-update) | async-done | bytes 2097168 | tf_op jit(solution)/shard_map/psum | solution.py:189
  339.8 6.1 multiply_convert_fusion
  348.7 6.8 fusion.2
  355.8 5.3 fusion.51
  367.3 11.8 %reduce-scatter.8.cloned.1.call-done = f32[2,256,256]{1,2,0:T(8,128)} async-done(((f32[2,1024,256]{1,2,0:T(8,128)}), f32[2,256,256]{1,2,0:T(8,128)}) %reduce-scatter.8.cloned.1.call-update) | async-done | bytes 524304 | tf_op jit(solution)/shard_map/reduce_scatter | solution.py:234
  382.7 30.6 %reduce-scatter.10.cloned.1.call-done = f32[2,256,256]{1,2,0:T(8,128)} async-done(((f32[2,1024,256]{1,2,0:T(8,128)}), f32[2,256,256]{1,2,0:T(8,128)}) %reduce-scatter.10.cloned.1.call-update) | async-done | bytes 524304 | tf_op jit(solution)/shard_map/reduce_scatter | solution.py:237
  422.7 153.9 %all-reduce.10.cloned.1.call-done = (f32[512,1024]{1,0:T(8,128)}, f32[512,1024]{1,0:T(8,128)}) async-done(((f32[512,1024]{1,0:T(8,128)}, f32[512,1024]{1,0:T(8,128)}), (f32[512,1024]{1,0:T(8,128)}, f32[512,1024]{1,0:T(8,128)})) %all-reduce.10.cloned.1.call-update) | async-done | bytes 4194320 | tf_op jit(solution)/shard_map/psum | solution.py:172
  579.9 4.3 convolution_bitcast_fusion
  587.4 5.3 fusion.50
  592.7 4.6 fusion.37
  597.5 14.4 %all-reduce = (f32[2,256]{1,0:T(2,128)}, f32[1024]{0:T(1024)}) all-reduce(f32[2,256]{1,0:T(2,128)S(1)} %pad_maximum_fusion.3, f32[1024]{0:T(1024)S(1)} %get-tuple-element.95), channel_id=1, replica_groups=mesh['shard'=2,'ctx'=4,'tp'=4] {'shard','ctx'}, use_global_device_ids=true, to_apply=%region_27.28 | all-reduce | flops 1536 | bytes 12288 | tf_op jit(solution)/shard_map/psum | solution.py:273
  618.7 41.6 %reduce-scatter.14.cloned.1.call-done = f32[3,128,256]{1,2,0:T(8,128)} async-done(((f32[3,1024,256]{1,2,0:T(8,128)}), f32[3,128,256]{1,2,0:T(8,128)}) %reduce-scatter.14.cloned.1.call-update) | async-done | bytes 393232 | tf_op jit(solution)/shard_map/reduce_scatter | solution.py:266
  662.2 38.2 %reduce-scatter.16.cloned.1.call-done = f32[128,256]{1,0:T(8,128)} async-done(((f32[1024,256]{1,0:T(8,128)}), f32[128,256]{1,0:T(8,128)}) %reduce-scatter.16.cloned.1.call-update) | async-done | bytes 131088 | tf_op jit(solution)/shard_map/reduce_scatter | solution.py:267
  700.4 55.5 %reduce-scatter.20.cloned.1.call-done = f32[128,1024]{1,0:T(8,128)} async-done(((f32[1024,1024]{1,0:T(8,128)}), f32[128,1024]{1,0:T(8,128)}) %reduce-scatter.20.cloned.1.call-update) | async-done | bytes 524304 | tf_op jit(solution)/shard_map/reduce_scatter | solution.py:269
  755.9 55.1 %reduce-scatter.18.cloned.1.call-done = f32[128,1024]{1,0:T(8,128)} async-done(((f32[1024,1024]{1,0:T(8,128)}), f32[128,1024]{1,0:T(8,128)}) %reduce-scatter.18.cloned.1.call-update) | async-done | bytes 524304 | tf_op jit(solution)/shard_map/reduce_scatter | solution.py:268
  (165 shorter events, 87.2 us)
Async XLA Ops:
  7.2 14.5 %copy-start = (bf16[2,256,1024]{2,1,0:T(8,128)(2,1)S(1)}, bf16[2,256,1024]{2,1,0:T(8,128)(2,1)}, u32[]{:S(2)}) copy-start(bf16[2,256,1024]{2,1,0:T(8,128)(2,1)} %param.15) | copy-start | bytes 3145732
  7.3 14.4 %copy-start.21 = (bf16[2,256]{1,0:T(2,128)(2,1)S(1)}, bf16[2,256]{1,0:T(2,128)(2,1)}, u32[]{:S(2)}) copy-start(bf16[2,256]{1,0:T(2,128)(2,1)} %param.21) | copy-start | bytes 3076
  7.3 31.2 %all-gather.6.cloned.1.call-start = ((), (), s32[]{:S(2)}) async-start(), calls=%async_computation.7 | async-start | bytes 1769472 | tf_op jit(solution)/shard_map/all_gather | solution.py:75
  8.0 50.8 %all-gather.10.cloned.1.call-start = ((), (), s32[]{:S(2)}) async-start(), calls=%async_computation.9 | async-start | bytes 1310720 | tf_op jit(solution)/shard_map/all_gather | solution.py:116
  23.1 19.0 %copy-start.20 = (bf16[128,256]{1,0:T(8,128)(2,1)S(1)}, bf16[128,256]{1,0:T(8,128)(2,1)}, u32[]{:S(2)}) copy-start(bf16[128,256]{1,0:T(8,128)(2,1)} %param.22) | copy-start | bytes 196612
  23.1 29.8 %copy-start.23 = (s32[2]{0:T(128)S(1)}, s32[2]{0:T(128)}, u32[]{:S(2)}) copy-start(s32[2]{0:T(128)} %param.16) | copy-start | bytes 28
  41.1 12.0 %copy-start.17 = (f32[3,512,256]{2,1,0:T(8,128)}, f32[3,512,256]{2,1,0:T(8,128)S(1)}, u32[]{:S(2)}) copy-start(f32[3,512,256]{2,1,0:T(8,128)S(1)} %convolution_bitcast_fusion.2) | copy-start | bytes 4718596
  42.0 35.8 %all-gather.8.cloned.1.call-start = ((), (), s32[]{:S(2)}) async-start(), calls=%async_computation.8 | async-start | bytes 1310720 | tf_op jit(solution)/shard_map/all_gather | solution.py:117
  53.4 25.8 %copy-start.14 = (pred[2,256,1024]{2,1,0:T(8,128)(4,1)}, pred[2,256,1024]{2,1,0:T(8,128)(4,1)S(1)}, u32[]{:S(2)}) copy-start(pred[2,256,1024]{2,1,0:T(8,128)(4,1)S(1)} %broadcast_and_fusion) | copy-start | bytes 1572868
  58.5 116.0 %all-reduce.6.cloned.1.call-start = ((), (), s32[]{:S(2)}) async-start(), calls=%async_computation.10 | async-start | bytes 4194304 | tf_op jit(solution)/shard_map/psum | solution.py:163
  79.3 6.7 copy-start.15
  87.8 115.4 %all-gather.12.cloned.1.call-start = ((), (), s32[]{:S(2)}) async-start(), calls=%async_computation.11 | async-start | bytes 2359296 | tf_op jit(solution)/shard_map/all_gather | solution.py:77
  88.4 144.7 %all-gather.14.cloned.1.call-start = ((), (), s32[]{:S(2)}) async-start(), calls=%async_computation.12 | async-start | bytes 2359296 | tf_op jit(solution)/shard_map/all_gather | solution.py:78
  89.0 239.5 %all-reduce.8.cloned.1.call-start = ((), (), s32[]{:S(2)}) async-start(), calls=%async_computation.13 | async-start | bytes 4194304 | tf_op jit(solution)/shard_map/psum | solution.py:189
  233.1 6.1 copy-start.30
  241.8 137.4 %reduce-scatter.8.cloned.1.call-start = ((), (), s32[]{:S(2)}) async-start(), calls=%async_computation.14 | async-start | bytes 2621440 | tf_op jit(solution)/shard_map/reduce_scatter | solution.py:234
  339.8 6.1 copy-start.13
  348.6 64.7 %reduce-scatter.10.cloned.1.call-start = ((), (), s32[]{:S(2)}) async-start(), calls=%async_computation.15 | async-start | bytes 2621440 | tf_op jit(solution)/shard_map/reduce_scatter | solution.py:237
  355.5 221.2 %all-reduce.10.cloned.1.call-start = ((), (), s32[]{:S(2)}) async-start(), calls=%async_computation.21 | async-start | bytes 8388608 | tf_op jit(solution)/shard_map/psum | solution.py:172
  421.2 196.1 %reduce-scatter.12.cloned.1.call-start = ((), (), s32[]{:S(2)}) async-start(), calls=%async_computation.16 | async-start | bytes 36864 | tf_op jit(solution)/shard_map/reduce_scatter | solution.py:270
  579.9 80.5 %reduce-scatter.14.cloned.1.call-start = ((), (), s32[]{:S(2)}) async-start(), calls=%async_computation.17 | async-start | bytes 3538944 | tf_op jit(solution)/shard_map/reduce_scatter | solution.py:266
  584.2 116.3 %reduce-scatter.16.cloned.1.call-start = ((), (), s32[]{:S(2)}) async-start(), calls=%async_computation.18 | async-start | bytes 1179648 | tf_op jit(solution)/shard_map/reduce_scatter | solution.py:267
  587.3 168.6 %reduce-scatter.20.cloned.1.call-start = ((), (), s32[]{:S(2)}) async-start(), calls=%async_computation.20 | async-start | bytes 4718592 | tf_op jit(solution)/shard_map/reduce_scatter | solution.py:269
  592.7 218.4 %reduce-scatter.18.cloned.1.call-start = ((), (), s32[]{:S(2)}) async-start(), calls=%async_computation.19 | async-start | bytes 4718592 | tf_op jit(solution)/shard_map/reduce_scatter | solution.py:268
  (23 other events, 78.2 us)
Sparse Core Ops, SparseCore 0:
  10.0 28.3 all-gather.5
  42.1 16.7 all-gather.9
  61.0 16.7 all-gather.7
  87.9 86.4 all-reduce.5
  176.4 26.8 all-gather.11
  205.2 27.8 all-gather.13
  241.9 86.5 all-reduce.7
  348.8 30.3 reduce-scatter.7
  381.9 31.4 reduce-scatter.9
  421.3 155.3 all-reduce.9
  580.5 30.2 reduce-scatter.11
  614.0 46.2 reduce-scatter.13
  664.4 36.0 reduce-scatter.15
  704.6 51.2 reduce-scatter.19
  759.7 51.3 reduce-scatter.17
where the time goes:
time: 819 us; the launch traced here: 818 us
  waiting for transfers between devices  639 us (78%)
  matrix products  69.5 us (8%)
  blocking collectives  35.5 us (4%)
  other arithmetic  31.6 us (4%)
  local copies, waits for them, and re-layouts  26.2 us (3%)
  between operations  14.5 us (2%)
    psum x1, waiting for transfers between devices, on_device(): mlp_sum = lax.psum(contract_last(hidden, down_full), 'tp')  154 us
    psum x1, waiting for transfers between devices, on_device(): back_two = lax.psum(contract_last(d_pre_bf, up_back), 'tp')  86.6 us
    psum x1, waiting for transfers between devices, on_device(): proj_sum = lax.psum(contract_last(attended, out_full), 'tp')  83.9 us
    reduce_scatter x1, waiting for transfers between devices, on_device(): lax.psum_scatter(grad_down, ('shard', 'ctx'), scatter_dimension=0, tiled=...  55.5 us
    reduce_scatter x1, waiting for transfers between devices, on_device(): lax.psum_scatter(grad_up, ('shard', 'ctx'), scatter_dimension=0, tiled=True)  55.1 us
    reduce_scatter x1, waiting for transfers between devices, on_device(): lax.psum_scatter(grad_qkv, ('shard', 'ctx'), scatter_dimension=1, tiled=T...  41.6 us
    reduce_scatter x1, waiting for transfers between devices, on_device(): lax.psum_scatter(grad_out, ('shard', 'ctx'), scatter_dimension=0, tiled=T...  38.2 us
    reduce_scatter x1, waiting for transfers between devices, on_device(): lax.psum_scatter(value_terms.reshape(groups, seq_len, head_width), 'ctx',...  30.6 us
  transfers between devices with their start and end apart: 15, of which 14 were waited for; matrix products, arithmetic and copies ran while one was open for 9% of the time, Pallas kernels for 0%

commit v1 on v0

--- a/solution.py
+++ b/solution.py
@@ -7,6 +7,22 @@
 HD = 64
 EPS = 1e-05
 KAPPA = math.sqrt(2.0 / math.pi)
+
+
+def gather_around(x, axis, dim):
+    ways, here, hop = (lax.axis_size(axis), lax.axis_index(axis), x.shape[dim])
+    shape = [n * ways if d == dim else n for d, n in enumerate(x.shape)]
+    full = lax.dynamic_update_slice_in_dim(jnp.zeros(shape, x.dtype), x, here * hop, axis=dim)
+    going_up = going_down = x
+    for far in range(1, ways // 2 + 1):
+        going_up = lax.ppermute(going_up, axis, [(d, (d + 1) % ways) for d in range(ways)])
+        full = lax.dynamic_update_slice_in_dim(full, going_up, (here - far) % ways * hop, axis=dim)
+        if 2 * far < ways:
+            going_down = lax.ppermute(going_down, axis, [(d, (d - 1) % ways) for d in range(ways)])
+            full = lax.dynamic_update_slice_in_dim(
+                full, going_down, (here + far) % ways * hop, axis=dim
+            )
+    return full
 
 
 def normalize(row, gain, shift):
@@ -74,7 +90,7 @@
     fetched = (
         lax.all_gather(w_qkv, ("shard", "ctx"), axis=1, tiled=True),
         lax.all_gather(w_out, ("shard", "ctx"), axis=0, tiled=True),
-        lax.all_gather(w_up, ("shard", "ctx"), axis=0, tiled=True),
+        gather_around(w_up, ("shard", "ctx"), 0),
         lax.all_gather(w_down, ("shard", "ctx"), axis=0, tiled=True),
         lax.all_gather(vectors, ("shard", "ctx"), axis=1, tiled=True),
     )

time: 819 us -> 815 us (level)
  waiting for transfers between devices: 639 us -> 622 us
    psum x1, waiting for transfers between devices: 83.9 us -> 57.6 us  [on_device(): proj_sum = lax.psum(contract_last(attended, out_full), 'tp')]
    ppermute x0 -> x7, waiting for transfers between devices: none -> 13 us  [the longest x4 12.1 us: gather_around(): lax.ppermute(going_up, axis, [(d, (d + 1) % ways) for d in range(ways)])]
  transfers between devices with their start and end apart: 15 -> 22, of which waited for: 14 -> 19; matrix products, arithmetic and copies ran while one was open for 9% -> 10% of each run, Pallas kernels for 0% -> 0%
where the time goes in v1:
time: 815 us; the launch traced here: 814 us
  waiting for transfers between devices  622 us (76%)
  matrix products  70.5 us (9%)
  blocking collectives  35.7 us (4%)
  local copies, waits for them, and re-layouts  31.3 us (4%)
  other arithmetic  30.6 us (4%)
  between operations  14.7 us (2%)
  starting transfers between devices  8.87 us (1%)
    psum x1, waiting for transfers between devices, on_device(): mlp_sum = lax.psum(contract_last(hidden, down_full), 'tp')  154 us
    psum x1, waiting for transfers between devices, on_device(): back_two = lax.psum(contract_last(d_pre_bf, up_back), 'tp')  86.6 us
    psum x1, waiting for transfers between devices, on_device(): proj_sum = lax.psum(contract_last(attended, out_full), 'tp')  57.6 us
    reduce_scatter x1, waiting for transfers between devices, on_device(): lax.psum_scatter(grad_up, ('shard', 'ctx'), scatter_dimension=0, tiled=True)  55.5 us
    reduce_scatter x1, waiting for transfers between devices, on_device(): lax.psum_scatter(grad_down, ('shard', 'ctx'), scatter_dimension=0, tiled=...  55.1 us
    reduce_scatter x1, waiting for transfers between devices, on_device(): lax.psum_scatter(grad_qkv, ('shard', 'ctx'), scatter_dimension=1, tiled=T...  41.5 us
    reduce_scatter x1, waiting for transfers between devices, on_device(): lax.psum_scatter(grad_out, ('shard', 'ctx'), scatter_dimension=0, tiled=T...  38.2 us
    reduce_scatter x1, waiting for transfers between devices, on_device(): lax.psum_scatter(value_terms.reshape(groups, seq_len, head_width), 'ctx',...  30.6 us
  transfers between devices with their start and end apart: 22, of which 19 were waited for; matrix products, arithmetic and copies ran while one was open for 10% of the time, Pallas kernels for 0%

profile of v1, /device:TPU:0, one launch (start us, length us, event | category | flops | bytes accessed | tf_op | source)
XLA Modules:
  0.0 814.1 jit_solution(11472103905745986510)
XLA Ops:
  11.3 10.3 %all_gather.27 = bf16[6,1024]{1,0:T(8,128)(2,1)S(1)} all-gather(bf16[6,128]{1,0:T(8,128)(2,1)S(1)} %stack.61), channel_id=1, replica_groups=mesh['shard'=2,'ctx'=4,'tp'=4] {'shard','ctx'}, dimensions={1}, use_global_device_ids=true | all-gather | bytes 13824 | tf_op jit(solution)/shard_map/all_gather | solution.py:95
  22.2 16.3 %all-gather.6.cloned.1.call-done = bf16[3,1024,256]{2,1,0:T(8,128)(2,1)} async-done(((bf16[3,128,256]{2,1,0:T(8,128)(2,1)}), bf16[3,1024,256]{2,1,0:T(8,128)(2,1)}) %all-gather.6.cloned.1.call-update) | async-done | bytes 1572880 | tf_op jit(solution)/shard_map/all_gather | solution.py:91
  42.9 10.9 %all_gather.31 = bf16[1024,256]{1,0:T(8,128)(2,1)} all-gather(bf16[128,256]{1,0:T(8,128)(2,1)S(1)} %copy-done.25), channel_id=1, replica_groups=mesh['shard'=2,'ctx'=4,'tp'=4] {'shard','ctx'}, dimensions={0}, use_global_device_ids=true | all-gather | bytes 589824 | tf_op jit(solution)/shard_map/all_gather | solution.py:92
  66.2 12.3 %all-gather.8.cloned.1.call-done = bf16[2,1024,256]{2,1,0:T(8,128)(2,1)} async-done(((bf16[2,256,256]{2,1,0:T(8,128)(2,1)}), bf16[2,1024,256]{2,1,0:T(8,128)(2,1)}) %all-gather.8.cloned.1.call-update) | async-done | bytes 1048592 | tf_op jit(solution)/shard_map/all_gather | solution.py:133
  80.0 6.0 fusion.31
  112.8 4.7 collective-permute-done.6
  117.6 57.6 %all-reduce.6.cloned.1.call-done = f32[512,1024]{1,0:T(8,128)} async-done(((f32[512,1024]{1,0:T(8,128)}), f32[512,1024]{1,0:T(8,128)}) %all-reduce.6.cloned.1.call-update) | async-done | bytes 2097168 | tf_op jit(solution)/shard_map/psum | solution.py:179
  181.4 22.6 %all-gather.12.cloned.1.call-done = bf16[1024,1024]{1,0:T(8,128)(2,1)} async-done(((bf16[128,1024]{1,0:T(8,128)(2,1)}), bf16[1024,1024]{1,0:T(8,128)(2,1)}) %all-gather.12.cloned.1.call-update) | async-done | bytes 2097168 | tf_op jit(solution)/shard_map/all_gather | solution.py:94
  204.0 5.9 fusion.60
  209.9 23.9 %all-gather.14.cloned.1.call-done = bf16[1024,1024]{1,0:T(8,128)(2,1)} async-done(((bf16[128,1024]{1,0:T(8,128)(2,1)}), bf16[1024,1024]{1,0:T(8,128)(2,1)}) %all-gather.14.cloned.1.call-update) | async-done | bytes 2097168 | tf_op jit(solution)/shard_map/all_gather | solution.py:193
  238.4 86.6 %all-reduce.8.cloned.1.call-done = f32[512,1024]{1,0:T(8,128)} async-done(((f32[512,1024]{1,0:T(8,128)}), f32[512,1024]{1,0:T(8,128)}) %all-reduce.8.cloned.1.call-update) | async-done | bytes 2097168 | tf_op jit(solution)/shard_map/psum | solution.py:205
  336.4 6.1 multiply_convert_fusion
  345.4 6.7 fusion.2
  352.3 5.3 fusion.51
  363.9 11.8 %reduce-scatter.8.cloned.1.call-done = f32[2,256,256]{1,2,0:T(8,128)} async-done(((f32[2,1024,256]{1,2,0:T(8,128)}), f32[2,256,256]{1,2,0:T(8,128)}) %reduce-scatter.8.cloned.1.call-update) | async-done | bytes 524304 | tf_op jit(solution)/shard_map/reduce_scatter | solution.py:250
  379.2 30.6 %reduce-scatter.10.cloned.1.call-done = f32[2,256,256]{1,2,0:T(8,128)} async-done(((f32[2,1024,256]{1,2,0:T(8,128)}), f32[2,256,256]{1,2,0:T(8,128)}) %reduce-scatter.10.cloned.1.call-update) | async-done | bytes 524304 | tf_op jit(solution)/shard_map/reduce_scatter | solution.py:253
  419.3 153.9 %all-reduce.10.cloned.1.call-done = (f32[512,1024]{1,0:T(8,128)}, f32[512,1024]{1,0:T(8,128)}) async-done(((f32[512,1024]{1,0:T(8,128)}, f32[512,1024]{1,0:T(8,128)}), (f32[512,1024]{1,0:T(8,128)}, f32[512,1024]{1,0:T(8,128)})) %all-reduce.10.cloned.1.call-update) | async-done | bytes 4194320 | tf_op jit(solution)/shard_map/psum | solution.py:188
  583.9 4.6 fusion.37
  588.6 5.3 fusion.50
  594.1 14.4 %all-reduce = (f32[2,256]{1,0:T(2,128)}, f32[1024]{0:T(1024)}) all-reduce(f32[2,256]{1,0:T(2,128)S(1)} %pad_maximum_fusion.3, f32[1024]{0:T(1024)S(1)} %get-tuple-element.95), channel_id=1, replica_groups=mesh['shard'=2,'ctx'=4,'tp'=4] {'shard','ctx'}, use_global_device_ids=true, to_apply=%region_27.28 | all-reduce | flops 1536 | bytes 12288 | tf_op jit(solution)/shard_map/psum | solution.py:289
  615.3 41.5 %reduce-scatter.14.cloned.1.call-done = f32[3,128,256]{1,2,0:T(8,128)} async-done(((f32[3,1024,256]{1,2,0:T(8,128)}), f32[3,128,256]{1,2,0:T(8,128)}) %reduce-scatter.14.cloned.1.call-update) | async-done | bytes 393232 | tf_op jit(solution)/shard_map/reduce_scatter | solution.py:282
  658.7 38.2 %reduce-scatter.16.cloned.1.call-done = f32[128,256]{1,0:T(8,128)} async-done(((f32[1024,256]{1,0:T(8,128)}), f32[128,256]{1,0:T(8,128)}) %reduce-scatter.16.cloned.1.call-update) | async-done | bytes 131088 | tf_op jit(solution)/shard_map/reduce_scatter | solution.py:283
  697.0 55.5 %reduce-scatter.18.cloned.1.call-done = f32[128,1024]{1,0:T(8,128)} async-done(((f32[1024,1024]{1,0:T(8,128)}), f32[128,1024]{1,0:T(8,128)}) %reduce-scatter.18.cloned.1.call-update) | async-done | bytes 524304 | tf_op jit(solution)/shard_map/reduce_scatter | solution.py:284
  752.5 55.1 %reduce-scatter.20.cloned.1.call-done = f32[128,1024]{1,0:T(8,128)} async-done(((f32[1024,1024]{1,0:T(8,128)}), f32[128,1024]{1,0:T(8,128)}) %reduce-scatter.20.cloned.1.call-update) | async-done | bytes 524304 | tf_op jit(solution)/shard_map/reduce_scatter | solution.py:285
  (194 shorter events, 112.9 us)
Async XLA Ops:
  7.3 31.2 %all-gather.6.cloned.1.call-start = ((), (), s32[]{:S(2)}) async-start(), calls=%async_computation.7 | async-start | bytes 1769472 | tf_op jit(solution)/shard_map/all_gather | solution.py:91
  8.0 51.6 %all-gather.10.cloned.1.call-start = ((), (), s32[]{:S(2)}) async-start(), calls=%async_computation.9 | async-start | bytes 1310720 | tf_op jit(solution)/shard_map/all_gather | solution.py:132
  22.1 31.6 %copy-start.28 = (s32[2]{0:T(128)S(1)}, s32[2]{0:T(128)}, u32[]{:S(2)}) copy-start(s32[2]{0:T(128)} %param.16) | copy-start | bytes 28
  42.7 35.8 %all-gather.8.cloned.1.call-start = ((), (), s32[]{:S(2)}) async-start(), calls=%async_computation.8 | async-start | bytes 1310720 | tf_op jit(solution)/shard_map/all_gather | solution.py:133
  58.1 117.1 %all-reduce.6.cloned.1.call-start = ((), (), s32[]{:S(2)}) async-start(), calls=%async_computation.10 | async-start | bytes 4194304 | tf_op jit(solution)/shard_map/psum | solution.py:179
  88.6 115.4 %all-gather.12.cloned.1.call-start = ((), (), s32[]{:S(2)}) async-start(), calls=%async_computation.11 | async-start | bytes 2359296 | tf_op jit(solution)/shard_map/all_gather | solution.py:94
  89.2 144.7 %all-gather.14.cloned.1.call-start = ((), (), s32[]{:S(2)}) async-start(), calls=%async_computation.12 | async-start | bytes 2359296 | tf_op jit(solution)/shard_map/all_gather | solution.py:193
  89.7 235.3 %all-reduce.8.cloned.1.call-start = ((), (), s32[]{:S(2)}) async-start(), calls=%async_computation.13 | async-start | bytes 4194304 | tf_op jit(solution)/shard_map/psum | solution.py:205
  89.8 7.0 collective-permute-start
  90.1 7.9 collective-permute-start.1
  96.8 7.1 collective-permute-start.2
  98.0 7.9 collective-permute-start.3
  103.9 7.0 collective-permute-start.4
  105.8 6.9 collective-permute-start.5
  110.9 6.7 collective-permute-start.6
  117.6 57.7 %copy-start.17 = (bf16[1024,1024]{1,0:T(8,128)(2,1)}, bf16[1024,1024]{1,0:T(8,128)(2,1)S(1)}, u32[]{:S(2)}) copy-start(bf16[1024,1024]{1,0:T(8,128)(2,1)S(1)} %constant_dynamic-update-slice_fusion) | copy-start | bytes 6291460
  238.4 137.3 %reduce-scatter.8.cloned.1.call-start = ((), (), s32[]{:S(2)}) async-start(), calls=%async_computation.14 | async-start | bytes 2621440 | tf_op jit(solution)/shard_map/reduce_scatter | solution.py:250
  345.1 64.7 %reduce-scatter.10.cloned.1.call-start = ((), (), s32[]{:S(2)}) async-start(), calls=%async_computation.15 | async-start | bytes 2621440 | tf_op jit(solution)/shard_map/reduce_scatter | solution.py:253
  352.2 221.0 %all-reduce.10.cloned.1.call-start = ((), (), s32[]{:S(2)}) async-start(), calls=%async_computation.21 | async-start | bytes 8388608 | tf_op jit(solution)/shard_map/psum | solution.py:188
  417.7 196.2 %reduce-scatter.12.cloned.1.call-start = ((), (), s32[]{:S(2)}) async-start(), calls=%async_computation.16 | async-start | bytes 36864 | tf_op jit(solution)/shard_map/reduce_scatter | solution.py:286
  576.4 80.5 %reduce-scatter.14.cloned.1.call-start = ((), (), s32[]{:S(2)}) async-start(), calls=%async_computation.17 | async-start | bytes 3538944 | tf_op jit(solution)/shard_map/reduce_scatter | solution.py:282
  580.7 116.3 %reduce-scatter.16.cloned.1.call-start = ((), (), s32[]{:S(2)}) async-start(), calls=%async_computation.18 | async-start | bytes 1179648 | tf_op jit(solution)/shard_map/reduce_scatter | solution.py:283
  583.9 168.6 %reduce-scatter.18.cloned.1.call-start = ((), (), s32[]{:S(2)}) async-start(), calls=%async_computation.19 | async-start | bytes 4718592 | tf_op jit(solution)/shard_map/reduce_scatter | solution.py:284
  588.5 219.1 %reduce-scatter.20.cloned.1.call-start = ((), (), s32[]{:S(2)}) async-start(), calls=%async_computation.20 | async-start | bytes 4718592 | tf_op jit(solution)/shard_map/reduce_scatter | solution.py:285
  (33 other events, 215.0 us)
Sparse Core Ops, SparseCore 0:
  10.0 28.3 all-gather.5
  42.8 16.7 all-gather.9
  61.8 16.7 all-gather.7
  88.7 86.4 all-reduce.5
  177.1 26.8 all-gather.11
  205.9 27.8 all-gather.13
  238.5 86.4 all-reduce.7
  345.3 30.3 reduce-scatter.7
  378.4 31.4 reduce-scatter.9
  417.8 155.3 all-reduce.9
  577.0 30.2 reduce-scatter.11
  610.6 46.2 reduce-scatter.13
  660.9 36.0 reduce-scatter.15
  701.1 51.2 reduce-scatter.17
  756.2 51.3 reduce-scatter.19
